TPU v7x, 256 devices: a whole 4x4x8 slice. The times are simulated.
256 devices in a mesh: fsdp: 256 (over z, x, y, core).
Axes of the slice: x: 4, y: 4, z: 8, core: 2. Of those that a mesh axis runs over, the one named last changes fastest.
Arguments:
- inputs: bfloat16 [256, 4096], P('fsdp'), may hold values from -6 to 6
- norm_gain: bfloat16 [4096], replicated, may hold values from 0.099609375 to 1.8984375
- lengths: int32 [2], replicated, may hold values from 1 to 128, 192 in all
- gate_rows: bfloat16 [10240, 4096], P('fsdp'), may hold values from -0.09375 to 0.09375
- up_rows: bfloat16 [10240, 4096], P('fsdp'), may hold values from -0.09375 to 0.09375
- down_rows: bfloat16 [10240, 4096], P('fsdp'), may hold values from -0.25 to 0.25
- krylov_gate: bfloat16 [8, 10240, 4096], P(None, 'fsdp'), may hold values from -30 to 30
- krylov_up: bfloat16 [8, 10240, 4096], P(None, 'fsdp'), may hold values from -30 to 30
- krylov_down: bfloat16 [8, 10240, 4096], P(None, 'fsdp'), may hold values from -30 to 30
Outputs:
- new_gate: bfloat16 [10240, 4096], P('fsdp')
- new_up: bfloat16 [10240, 4096], P('fsdp')
- new_down: bfloat16 [10240, 4096], P('fsdp')
- coefficients: float32 [9], replicated
Inputs may be any that keep to these rules, and one draw needn't show every extreme that they name: The lengths sum to exactly 192.
All inputs are finite; a program needn't handle non-finite values.
Results may differ from a plain program's by a relative error of at most 0.0051.
The roundings to bfloat16 on the way count: a program that leaves them out, or rounds other values in their place, can miss the bound.
Values may be sent and summed in bfloat16 or wider, within the bound.
A program may use at most 64 MiB of HBM per device.

v0:
```python
import math

import jax
import jax.numpy as jnp
from jax import lax
from jax.sharding import PartitionSpec as P

LEN = 128


def gelu_pair(gate_pre):
    coef = math.sqrt(2.0 / math.pi)
    cube = gate_pre * gate_pre * gate_pre
    tanh_val = jnp.tanh(coef * (gate_pre + 0.044715 * cube))
    act = 0.5 * gate_pre * (1.0 + tanh_val)
    slope = 0.5 * (1.0 + tanh_val) + 0.5 * gate_pre * (1.0 - tanh_val * tanh_val) * coef * (
        1.0 + 3.0 * 0.044715 * gate_pre * gate_pre
    )
    return (act, slope)


def contract_first(left, right):
    return lax.dot_general(
        left, right, (((0,), (0,)), ((), ())), preferred_element_type=jnp.float32
    )


def contract_last(left, right):
    return lax.dot_general(
        left, right, (((1,), (1,)), ((), ())), preferred_element_type=jnp.float32
    )


def live_mask(positions, lengths):
    seq_ids = positions // LEN
    table = jnp.arange(lengths.shape[0], dtype=jnp.int32)
    limits = jnp.sum(jnp.where(seq_ids[:, None] == table[None, :], lengths[None, :], 0), axis=1)
    return (positions % LEN < limits).astype(jnp.float32)


def local_dots(parts, grads):
    total = jnp.zeros((parts[0].shape[0],), jnp.float32)
    for krylov, grad in zip(parts, grads):
        total = total + jnp.einsum(
            "jfd,fd->j", krylov.astype(jnp.float32), grad, precision=lax.Precision.HIGHEST
        )
    return total


def per_device(
    inputs, norm_gain, lengths, gate_rows, up_rows, down_rows, krylov_gate, krylov_up, krylov_down
):
    parts = (krylov_gate, krylov_up, krylov_down)
    basis_count = krylov_gate.shape[0]
    width = inputs.shape[1]
    devices = lax.axis_size("fsdp")
    hidden_all = gate_rows.shape[0] * devices
    count = 3.0 * width * hidden_all
    wide = inputs.astype(jnp.float32)
    normed_own = (
        wide
        * lax.rsqrt(jnp.mean(wide * wide, axis=1, keepdims=True) + 1e-06)
        * norm_gain.astype(jnp.float32)
    ).astype(jnp.bfloat16)
    normed = lax.all_gather(normed_own, "fsdp", axis=0, tiled=True)
    token_count = normed.shape[0]
    inv_d = 1.0 / math.sqrt(width)
    inv_ff = 1.0 / math.sqrt(hidden_all)
    probe_gate = krylov_gate[basis_count - 1]
    probe_up = krylov_up[basis_count - 1]
    probe_down = krylov_down[basis_count - 1]
    gate_pre = contract_last(gate_rows, normed)
    up_pre = contract_last(up_rows, normed)
    tan_gate = contract_last(probe_gate, normed) * inv_d
    tan_up = contract_last(probe_up, normed) * inv_d
    act, slope = gelu_pair(gate_pre)
    hidden = (act * up_pre).astype(jnp.bfloat16)
    tangent = (slope * tan_gate * up_pre + act * tan_up).astype(jnp.bfloat16)
    jvp_own = lax.psum_scatter(
        contract_first(down_rows, tangent) + contract_first(probe_down, hidden) * inv_ff,
        "fsdp",
        scatter_dimension=0,
        tiled=True,
    )
    live = live_mask(jnp.arange(token_count, dtype=jnp.int32), lengths)
    loss_own = (jvp_own * live[None, :]).astype(jnp.bfloat16)
    loss_t = lax.all_gather(loss_own, "fsdp", axis=0, tiled=True)
    back = jnp.dot(down_rows, loss_t, preferred_element_type=jnp.float32)
    grad_down = contract_last(hidden, loss_t) * inv_ff
    s_term = (back * up_pre * slope).astype(jnp.bfloat16)
    r_term = (back * act).astype(jnp.bfloat16)
    grad_gate = jnp.dot(s_term, normed, preferred_element_type=jnp.float32) * inv_d
    grad_up = jnp.dot(r_term, normed, preferred_element_type=jnp.float32) * inv_d
    grads = (grad_gate, grad_up, grad_down)
    dots_own = local_dots(parts, grads)
    proj = lax.psum(dots_own, "fsdp") / count
    residuals = []
    for krylov, grad in zip(parts, grads):
        residuals.append(
            grad
            - jnp.einsum(
                "j,jfd->fd", proj, krylov.astype(jnp.float32), precision=lax.Precision.HIGHEST
            )
        )
    own_left = (
        jnp.sum(residuals[0] * residuals[0])
        + jnp.sum(residuals[1] * residuals[1])
        + jnp.sum(residuals[2] * residuals[2])
    )
    squares = lax.psum(own_left, "fsdp") / count
    norm = jnp.sqrt(squares + 1e-06)
    new_gate = (residuals[0] / norm).astype(jnp.bfloat16)
    new_up = (residuals[1] / norm).astype(jnp.bfloat16)
    new_down = (residuals[2] / norm).astype(jnp.bfloat16)
    coefficients = jnp.concatenate([proj, norm[None]])
    return (new_gate, new_up, new_down, coefficients)


def solution(mesh):
    placed = (
        P("fsdp", None),
        P(),
        P(),
        P("fsdp", None),
        P("fsdp", None),
        P("fsdp", None),
        P(None, "fsdp", None),
        P(None, "fsdp", None),
        P(None, "fsdp", None),
    )
    return jax.shard_map(
        per_device,
        mesh=mesh,
        in_specs=placed,
        out_specs=(P("fsdp", None), P("fsdp", None), P("fsdp", None), P()),
        check_vma=False,
    )
```

profile of v0, /device:TPU:1, one launch (start us, length us, event | category | flops | bytes accessed | tf_op | source)
XLA Modules:
  0.0 1762.4 jit_solution(11164698938398851685)
XLA Ops:
  7.2 0.0 copy-start
  7.2 0.0 all-gather.6.cloned.1.call-start
  7.2 0.7 broadcast_in_dim.31
  8.0 1.4 multiply_reduce_fusion.3
  10.0 1.4 convert_bitcast_fusion
  11.4 0.0 all-gather.6.cloned.1.call-update
  11.4 0.0 copy-start.11
  11.4 0.0 reduce-scatter.4.cloned.1.call-start
  11.4 120.8 %all-gather.6.cloned.1.call-done = bf16[256,1,4096]{2,1,0:T(2,128)(2,1)} async-done(((bf16[1,1,4096]{2,1,0:T(2,128)(2,1)}), bf16[256,1,4096]{2,1,0:T(2,128)(2,1)}) %all-gather.6.cloned.1.call-update) | async-done | bytes 2097168 | tf_op jit(solution)/shard_map/all_gather | solution.py:65
  132.2 4.5 copy.27
  136.7 0.0 copy-done.11
  136.8 0.0 copy-start.12
  136.8 0.7 fusion.23
  137.5 0.2 copy-done.12
  137.7 0.7 multiply_convert_fusion.2
  138.5 1.7 fusion.50
  140.2 3.7 convolution_multiply_fusion
  143.9 0.0 copy-done
  143.9 6.8 fusion
  150.6 5.6 copy.25
  156.2 0.0 reduce-scatter.4.cloned.1.call-update
  156.3 0.3 all-gather.4.cloned.1.call-start
  156.6 0.3 copy-done.13
  156.9 0.1 fusion.92
  157.0 1281.2 %reduce-scatter.4.cloned.1.call-done = f32[16,256]{1,0:T(8,128)} async-done(((f32[4096,256]{1,0:T(8,128)}), f32[16,256]{1,0:T(8,128)}) %reduce-scatter.4.cloned.1.call-update) | async-done | bytes 16400 | tf_op jit(solution)/shard_map/reduce_scatter | solution.py:79
  1438.2 1.3 multiply_convert_fusion.5
  1439.5 0.0 all-gather.4.cloned.1.call-update
  1439.5 106.8 %all-gather.4.cloned.1.call-done = bf16[4096,256]{1,0:T(8,128)(2,1)} async-done(((bf16[16,256]{1,0:T(8,128)(2,1)}), bf16[4096,256]{1,0:T(8,128)(2,1)}) %all-gather.4.cloned.1.call-update) | async-done | bytes 2097168 | tf_op jit(solution)/shard_map/all_gather | solution.py:87
  1546.4 2.0 convolution_bitcast_fusion
  1548.4 0.0 copy-start.7
  1548.4 0.5 convolution_multiply_fusion.3
  1548.9 0.5 convolution_multiply_fusion.2
  1549.4 0.0 copy-start.2
  1549.4 0.0 copy-start.9
  1549.4 0.8 copy-done.7
  1550.2 8.5 fusion.58
  1558.7 0.0 copy-done.9
  1558.7 9.3 fusion.70
  1568.0 0.0 copy-done.2
  1568.0 0.0 copy-done.1
  1568.0 0.0 copy-start.10
  1568.0 0.7 convolution_multiply_fusion.1
  1568.7 1.0 copy-done.10
  1569.7 8.8 fusion.67
  1578.5 77.1 %psum.14 = f32[8]{0:T(128)S(1)} all-reduce(f32[8]{0:T(128)S(1)} %fusion.67), channel_id=1, replica_groups=mesh['fsdp'=256] {'fsdp'}, use_global_device_ids=true, to_apply=%region_3.4 | all-reduce | flops 8 | bytes 64 | tf_op jit(solution)/shard_map/psum | solution.py:96
  1655.6 0.0 copy-start.8
  1655.6 6.5 fusion.1
  1662.1 6.4 fusion.5
  1668.5 0.0 copy-done.8
  1668.5 0.0 copy-start.6
  1668.5 0.0 copy-start.3
  1668.5 4.8 fusion.9
  1673.4 0.0 copy-start.4
  1673.4 1.0 multiply_reduce_fusion
  1674.4 0.0 copy-done.4
  1674.4 0.0 copy-done.3
  1674.4 1.4 multiply_reduce_fusion.1
  1675.8 0.0 copy-done.6
  1677.7 72.2 %psum.15 = f32[]{:T(128)} all-reduce(f32[]{:T(128)S(6)} %add.74), channel_id=1, replica_groups=mesh['fsdp'=256] {'fsdp'}, use_global_device_ids=true, to_apply=%region_7.8 | all-reduce | flops 1 | bytes 8 | tf_op jit(solution)/shard_map/psum | solution.py:110
  1750.6 0.0 copy-start.5
  1750.6 1.1 divide_convert_fusion
  1751.7 2.2 divide_convert_fusion.1
  1753.9 1.1 divide_convert_fusion.2
  1755.0 0.6 pad_maximum_fusion
  (6 shorter events, 0.0 us)
Async XLA Ops:
  7.2 136.7 %copy-start = (bf16[40,4096]{1,0:T(8,128)(2,1)S(1)}, bf16[40,4096]{1,0:T(8,128)(2,1)}, u32[]{:S(2)}) copy-start(bf16[40,4096]{1,0:T(8,128)(2,1)} %param.14) | copy-start | bytes 983044
  7.2 125.0 %all-gather.6.cloned.1.call-start = ((), (), s32[]{:S(2)}) async-start(), calls=%async_computation.2 | async-start | bytes 4210688 | tf_op jit(solution)/shard_map/all_gather | solution.py:65
  11.4 125.4 %copy-start.11 = (bf16[40,4096]{1,0:T(8,128)(2,1)S(1)}, bf16[40,4096]{1,0:T(8,128)(2,1)}, u32[]{:S(2)}) copy-start(bf16[40,4096]{1,0:T(8,128)(2,1)} %param.12) | copy-start | bytes 983044
  11.4 1426.8 %reduce-scatter.4.cloned.1.call-start = ((), (), s32[]{:S(2)}) async-start(), calls=%async_computation.3 | async-start | bytes 4210688 | tf_op jit(solution)/shard_map/reduce_scatter | solution.py:79
  136.8 1.0 copy-start.12
  156.2 0.7 copy-start.13
  156.3 1390.1 %all-gather.4.cloned.1.call-start = ((), (), s32[]{:S(2)}) async-start(), calls=%async_computation.1 | async-start | bytes 2105344 | tf_op jit(solution)/shard_map/all_gather | solution.py:87
  1548.4 1.7 copy-start.7
  1549.4 18.6 %copy-start.2 = (f32[40,4096]{1,0:T(8,128)}, f32[40,4096]{1,0:T(8,128)S(1)}, u32[]{:S(2)}) copy-start(f32[40,4096]{1,0:T(8,128)S(1)} %convolution_multiply_fusion.2) | copy-start | bytes 1966084
  1549.4 9.3 copy-start.9
  1558.7 9.3 copy-start.1
  1568.0 1.7 copy-start.10
  1655.6 12.9 copy-start.8
  1668.5 7.3 copy-start.6
  1668.5 5.9 copy-start.3
  1673.4 1.0 copy-start.4
  1750.6 3.3 copy-start.5
Sparse Core Ops, SparseCore 0:
  12.3 119.9 all-gather.5
  156.4 1281.7 reduce-scatter.3
  1442.5 103.8 all-gather.3
where the time goes:
time: 1770 us; the launch traced here: 1760 us
  waiting for transfers between devices  1510 us (85%)
  blocking collectives  149 us (8%)
  matrix products  61.5 us (3%)
    reduce_scatter x1, waiting for transfers between devices, per_device(): lax.psum_scatter(contract_first(down_rows, tangent) + contract_first(prob...  1280 us
    all_gather x1, waiting for transfers between devices, per_device(): normed = lax.all_gather(normed_own, 'fsdp', axis=0, tiled=True)  121 us
    all_gather x1, waiting for transfers between devices, per_device(): loss_t = lax.all_gather(loss_own, 'fsdp', axis=0, tiled=True)  107 us
    psum x1, blocking collectives, per_device(): proj = lax.psum(dots_own, 'fsdp') / count  77.1 us
    psum x1, blocking collectives, per_device(): squares = lax.psum(own_left, 'fsdp') / count  72.2 us
  transfers between devices with their start and end apart: 3, of which 3 were waited for; matrix products, arithmetic and copies ran while one was open for 0% of the time, Pallas kernels for 0%

commit v1 on v0

v1 whole, which is shorter than its diff:
```python
import functools
import math

import jax
import jax.numpy as jnp
from jax import lax
from jax.experimental import pallas as pl
from jax.experimental.pallas import tpu as pltpu
from jax.sharding import PartitionSpec as P

MESH = pl.DeviceIdType.MESH
F32 = jnp.float32
BF16 = jnp.bfloat16
GRAM = 16


def sides(devices):
    return {256: (8, 4), 16: (2, 2)}[devices]


def gelu_pair(gate_pre):
    coef = math.sqrt(2.0 / math.pi)
    cube = gate_pre * gate_pre * gate_pre
    tanh_val = jnp.tanh(coef * (gate_pre + 0.044715 * cube))
    act = 0.5 * gate_pre * (1.0 + tanh_val)
    slope = 0.5 * (1.0 + tanh_val) + 0.5 * gate_pre * (1.0 - tanh_val * tanh_val) * coef * (
        1.0 + 3.0 * 0.044715 * gate_pre * gate_pre
    )
    return (act, slope)


def mm(left, right):
    return jnp.dot(left, right, preferred_element_type=F32)


def mm_last(left, right):
    return lax.dot_general(left, right, (((1,), (1,)), ((), ())), preferred_element_type=F32)


def fold(value):
    rows = value.shape[0]
    total = value[0:8]
    for start in range(8, rows, 8):
        total = total + value[start : start + 8]
    return total


def body(
    cfg,
    len_ref,
    x_hbm,
    gain_hbm,
    gate_hbm,
    up_hbm,
    down_hbm,
    kg_hbm,
    ku_hbm,
    kd_hbm,
    og_hbm,
    ou_hbm,
    od_hbm,
    coef_ref,
    x_v,
    gain_v,
    gate_v,
    up_v,
    down_v,
    k_v,
    rowbuf,
    rows32,
    tok,
    w4,
    sel,
    nc,
    pre,
    psend,
    precv,
    own,
    asend,
    arecv,
    bsend,
    brecv,
    zsum,
    zrecv,
    lz,
    loss,
    backacc,
    w_v,
    gacc,
    qrows,
    sc_p,
    sc_x,
    sc_y,
    sc_z,
    sc_v,
    out_v,
    lsem,
    ksem,
    osem,
    s1,
    r1,
    s2,
    r2,
    s3,
    r3,
):
    Z, A, D, T, L, F, BASIS = cfg
    H = D // 2
    W = H // A
    RZ = L // Z
    R = D // 128
    CH = min(512, D)
    LEN = T // 2
    inv_d = 1.0 / math.sqrt(D)
    inv_ff = 1.0 / math.sqrt(F * T)
    inv_count = 1.0 / (3.0 * D * F * T)
    plane = 2 * A * A

    me = lax.axis_index("fsdp")
    c = lax.rem(me, 2)
    y = lax.rem(me // 2, A)
    x = lax.rem(me // (2 * A), A)
    z = me // plane
    sa = 2 * A - (2 * A - 2) * c
    sb = 2 + (2 * A - 2) * c
    a = x + c * (y - x)
    b = y + c * (x - y)
    partner = me + 1 - 2 * c

    def step(i, k, n):
        return lax.rem(i + k, n)

    def back_of(i, k, n):
        return lax.rem(i + n - k, n)

    def dev_z(k):
        return me + (step(z, k, Z) - z) * plane

    def dev_a(k):
        return me + (step(a, k, A) - a) * sa

    def dev_b(k):
        return me + (step(b, k, A) - b) * sb

    def dev_x(k):
        return me + (step(x, k, A) - x) * (2 * A)

    def dev_y(k):
        return me + (step(y, k, A) - y) * 2

    pending = []

    def send(src, dst, ss, rs, dev):
        cp = pltpu.make_async_remote_copy(
            src_ref=src, dst_ref=dst, send_sem=ss, recv_sem=rs, device_id=(dev,), device_id_type=MESH
        )
        cp.start()
        pending.append(cp)
        return cp

    loads = []
    for i, (src, dst) in enumerate(
        ((x_hbm, x_v), (gain_hbm, gain_v), (gate_hbm, gate_v), (up_hbm, up_v), (down_hbm, down_v))
    ):
        cp = pltpu.make_async_copy(src, dst, lsem.at[i])
        cp.start()
        loads.append(cp)
    kloads = []
    for i, src in enumerate((kg_hbm, ku_hbm, kd_hbm)):
        cp = pltpu.make_async_copy(src, k_v.at[i], ksem.at[i])
        cp.start()
        kloads.append(cp)

    barrier = pltpu.get_barrier_semaphore()
    peers = [dev_z(k) for k in range(1, Z)]
    peers += [dev_a(k) for k in range(1, A)] + [dev_b(k) for k in range(1, A)] + [partner]
    for peer in peers:
        pl.semaphore_signal(barrier, inc=1, device_id=(peer,), device_id_type=MESH)

    loads[0].wait()
    loads[1].wait()
    wide = x_v[...].astype(F32)
    square = jnp.sum(jnp.sum(wide * wide, axis=1, keepdims=True), axis=0, keepdims=True)
    normed_own = wide * lax.rsqrt(square * (1.0 / D) + 1e-06) * gain_v[...].astype(F32)
    rowbuf[z, a] = normed_own.astype(BF16)

    gacc[...] = jnp.zeros_like(gacc)

    def gram(part):
        def chunk(i, carry):
            cols = pl.ds(pl.multiple_of(i * 128, 128), 128)
            ks = [k_v[part, j, :, cols].astype(F32) for j in range(BASIS)]
            n = 0
            for i1 in range(BASIS):
                for j1 in range(i1, BASIS):
                    gacc[n] += fold(ks[i1] * ks[j1])
                    n += 1
            return carry

        lax.fori_loop(0, D // 128, chunk, 0)

    pl.semaphore_wait(barrier, len(peers))

    cps = []
    for k in range(1, Z):
        cps.append(send(rowbuf.at[z, a], rowbuf.at[z, a], s1.at[k - 1], r1.at[k - 1], dev_z(k)))
    kloads[0].wait()
    gram(0)
    for cp in cps:
        cp.wait_recv()
    cps = []
    o = Z - 1
    for k in range(1, A):
        cps.append(
            send(rowbuf.at[:, a], rowbuf.at[:, a], s1.at[o + k - 1], r1.at[o + k - 1], dev_a(k))
        )
    kloads[1].wait()
    gram(1)
    for cp in cps:
        cp.wait_recv()
    for i in range(Z):
        for j in range(A):
            rows32[pl.ds((i * A + j) * R, R), :] = rowbuf[i, j].astype(F32)
    for d in range(R):
        tok[c, b, :, pl.ds(d * 128, 128)] = rows32[pl.ds(d, Z * A, stride=R), :].astype(BF16)
    cps = []
    o += A - 1
    for k in range(1, A):
        cps.append(send(tok.at[c, b], tok.at[c, b], s1.at[o + k - 1], r1.at[o + k - 1], dev_b(k)))
    o += A - 1
    pairs = [send(tok.at[c, b], tok.at[c, b], s1.at[o], r1.at[o], partner)]
    kloads[2].wait()
    gram(2)
    loads[2].wait()
    loads[3].wait()
    loads[4].wait()

    def stack(i, carry):
        cols = pl.ds(pl.multiple_of(i * CH, CH), CH)
        parts = [gate_v[:, cols], up_v[:, cols], k_v[0, BASIS - 1, :, cols], k_v[1, BASIS - 1, :, cols]]
        w4[:, cols] = jnp.concatenate([p.astype(F32) for p in parts], axis=0).astype(BF16)
        return carry

    lax.fori_loop(0, D // CH, stack, 0)
    len0 = len_ref[0]
    len1 = len_ref[1]
    col = lax.broadcasted_iota(jnp.int32, (L, T), 1)
    row = lax.broadcasted_iota(jnp.int32, (L, T), 0)
    gc = col // (T // 2)
    gb = lax.rem(col // (Z * A), A)
    gz = lax.rem(col // A, Z)
    ga = lax.rem(col, A)
    gx = ga + gc * (gb - ga)
    gy = gb + gc * (ga - gb)
    token = gz * plane + gx * (2 * A) + gy * 2 + gc
    second = token >= LEN
    inner = jnp.where(second, token - LEN, token)
    live = inner < jnp.where(second, len1, len0)
    place = jnp.where(live, inner + jnp.where(second, len0, 0), -1)
    hit = place == row
    sel[...] = jnp.where(hit, 1.0, 0.0).astype(BF16)
    for k in range(1, A):
        cps[k - 1].wait_recv()
        kb = back_of(b, k, A)
        pairs.append(send(tok.at[c, kb], tok.at[c, kb], s1.at[o + k], r1.at[o + k], partner))
    for cp in pairs:
        cp.wait_recv()

    pre[...] = jnp.zeros_like(pre)

    def first(i, carry):
        cols = pl.ds(pl.multiple_of(i * CH, CH), CH)
        every = tok[:, :, :, cols].reshape(T, CH)
        kept = mm(sel[...], every).astype(BF16)
        nc[:, cols] = kept
        pre[...] += mm_last(w4[:, cols], kept)
        return carry

    lax.fori_loop(0, D // CH, first, 0)
    gate_pre = pre[0:F]
    up_pre = pre[F : 2 * F]
    tan_gate = pre[2 * F : 3 * F] * inv_d
    tan_up = pre[3 * F : 4 * F] * inv_d
    act, slope = gelu_pair(gate_pre)
    hidden = act * up_pre
    tangent = slope * tan_gate * up_pre + act * tan_up
    hid_t = hidden.T.astype(BF16)
    tan_t = tangent.T.astype(BF16)

    def jvp_block(start):
        cols = pl.ds(pl.multiple_of(start, 128), W)
        return mm(tan_t, down_v[:, cols]) + mm(hid_t, k_v[2, BASIS - 1, :, cols]) * inv_ff

    order = list(range(1, A)) + [0]
    pcps = [None] * A
    for k in order:
        psend[k] = jvp_block((1 - c) * H + step(b, k, A) * W).astype(BF16)
        pcps[k] = send(psend.at[k], precv.at[k], s2.at[k], r2.at[k], partner)
    o = A
    for k in order:
        own[k] = jvp_block(c * H + step(a, k, A) * W)
    acps = []
    for k in order:
        pcps[k].wait_recv()
        total = own[k] + precv[k].astype(F32)
        if k:
            asend[k - 1] = total.astype(BF16)
            acps.append(send(asend.at[k - 1], arecv.at[k - 1], s2.at[o + k - 1], r2.at[o + k - 1], dev_a(k)))
        else:
            own[0] = total
    o += A - 1
    for cp in acps:
        cp.wait_recv()
    bcps = []
    for k in order:
        cols = pl.ds(pl.multiple_of(step(b, k, A) * 128, 128), 128)
        total = own[0, :, cols]
        for j in range(A - 1):
            total = total + arecv[j, :, cols].astype(F32)
        if k:
            bsend[k - 1] = total.astype(BF16)
            bcps.append(send(bsend.at[k - 1], brecv.at[k - 1], s2.at[o + k - 1], r2.at[o + k - 1], dev_b(k)))
        else:
            kept = total
    o += A - 1
    for cp in bcps:
        cp.wait_recv()
    for j in range(A - 1):
        kept = kept + brecv[j].astype(F32)
    zsum[...] = kept
    zcps = []
    for k in range(1, Z):
        rows = pl.ds(pl.multiple_of(step(z, k, Z) * RZ, RZ), RZ)
        zcps.append(send(zsum.at[rows], zrecv.at[k - 1], s2.at[o + k - 1], r2.at[o + k - 1], dev_z(k)))
    o += Z - 1
    mine = pl.ds(pl.multiple_of(z * RZ, RZ), RZ)
    for cp in zcps:
        cp.wait_recv()
    total = zsum[mine, :]
    for j in range(Z - 1):
        total = total + zrecv[j]
    lz[mine, :] = total.astype(BF16).astype(F32)

    zcps = []
    for k in range(1, Z):
        zcps.append(send(lz.at[mine], lz.at[mine], s3.at[k - 1], r3.at[k - 1], dev_z(k)))
    o = Z - 1
    for cp in zcps:
        cp.wait_recv()

    def block(ai, bi):
        return pl.ds(pl.multiple_of(c * H + ai * W + bi * 128, 128), 128)

    here = block(a, b)
    loss[:, here] = lz[...].astype(BF16)
    bcps = []
    for k in range(1, A):
        bcps.append(send(loss.at[:, here], loss.at[:, here], s3.at[o + k - 1], r3.at[o + k - 1], dev_b(k)))
    o += A - 1
    oa = o
    op = oa + A * (A - 1)
    acps = {}
    gcps = {}

    def pass_on(kb):
        ref = loss.at[:, block(a, back_of(b, kb, A))]
        for k in range(1, A):
            n = oa + kb * (A - 1) + k - 1
            acps[k, kb] = send(ref, ref, s3.at[n], r3.at[n], dev_a(k))
        gcps[0, kb] = send(ref, ref, s3.at[op + kb], r3.at[op + kb], partner)

    pass_on(0)
    for kb in range(1, A):
        bcps[kb - 1].wait_recv()
        pass_on(kb)
    for kb in range(A):
        for ka in range(1, A):
            acps[ka, kb].wait_recv()
            ref = loss.at[:, block(back_of(a, ka, A), back_of(b, kb, A))]
            n = op + ka * A + kb
            gcps[ka, kb] = send(ref, ref, s3.at[n], r3.at[n], partner)
    o = op + A * A
    for kb in range(A):
        for ka in range(A):
            gcps[ka, kb].wait_recv()

    backacc[...] = jnp.zeros_like(backacc)

    def second_pass(i, carry):
        cols = pl.ds(pl.multiple_of(i * CH, CH), CH)
        backacc[...] += mm_last(down_v[:, cols], loss[:, cols])
        return carry

    lax.fori_loop(0, D // CH, second_pass, 0)
    back = backacc[...]
    gate_pre = pre[0:F]
    up_pre = pre[F : 2 * F]
    act, slope = gelu_pair(gate_pre)
    hid = (act * up_pre).astype(BF16)
    both = jnp.concatenate([back * up_pre * slope, back * act], axis=0).astype(BF16)

    def grads(i, carry):
        cols = pl.ds(pl.multiple_of(i * CH, CH), CH)
        two = mm(both, nc[:, cols]) * inv_d
        three = mm(hid, loss[:, cols]) * inv_ff
        parts = (two[0:F], two[F : 2 * F], three)
        carry = list(carry)
        for part in range(3):
            grad = parts[part]
            w_v[part, :, cols] = grad
            for sub in range(CH // 128):
                g = grad[:, sub * 128 : (sub + 1) * 128]
                scols = pl.ds(pl.multiple_of(i * CH + sub * 128, 128), 128)
                for j in range(BASIS):
                    carry[j] = carry[j] + fold(k_v[part, j, :, scols].astype(F32) * g)
                carry[BASIS] = carry[BASIS] + fold(g * g)
        return tuple(carry)

    zero = jnp.zeros((8, 128), F32)
    sums = lax.fori_loop(0, D // CH, grads, (zero,) * (BASIS + 1))
    qrows[...] = jnp.zeros_like(qrows)
    for j in range(BASIS + 1):
        qrows[j : j + 1, :] = jnp.sum(sums[j], axis=0, keepdims=True)
    n = 0
    for i1 in range(BASIS):
        for j1 in range(i1, BASIS):
            q = GRAM + i1 * BASIS + j1
            qrows[q : q + 1, :] = jnp.sum(gacc[n], axis=0, keepdims=True)
            n += 1
    line = jnp.sum(qrows[...], axis=1, keepdims=True) * inv_count
    rowi = lax.broadcasted_iota(jnp.int32, (128, 128), 0)
    coli = lax.broadcasted_iota(jnp.int32, (128, 128), 1)
    tile = jnp.sum(jnp.where(rowi == coli, line, 0.0), axis=0, keepdims=True)
    tile = jnp.broadcast_to(tile, (8, 128))

    def share(slots, value, at, size, o, dev):
        slots[at] = value
        cps = []
        for k in range(1, size):
            cps.append(send(slots.at[at], slots.at[at], s3.at[o + k - 1], r3.at[o + k - 1], dev(k)))
        for cp in cps:
            cp.wait_recv()
        total = slots[0]
        for j in range(1, size):
            total = total + slots[j]
        return total

    tile = share(sc_p, tile, c, 2, o, lambda k: partner)
    o += 1
    tile = share(sc_x, tile, x, A, o, dev_x)
    o += A - 1
    tile = share(sc_y, tile, y, A, o, dev_y)
    o += A - 1
    tile = share(sc_z, tile, z, Z, o, dev_z)
    o += Z - 1

    tile = tile[0:1]
    lane = lax.broadcasted_iota(jnp.int32, (1, 128), 1)
    proj = [
        jnp.sum(jnp.where(lane == j, tile, 0.0), axis=1, keepdims=True) for j in range(BASIS)
    ]
    gi = (lane - GRAM) // BASIS
    gj = lax.rem(lane + (8 * BASIS - GRAM), BASIS)
    left = jnp.zeros_like(tile)
    right = jnp.zeros_like(tile)
    for j in range(BASIS):
        left = left + jnp.where(gi == j, proj[j], 0.0)
        right = right + jnp.where(gj == j, proj[j], 0.0)
    inside = (lane >= GRAM) & (lane < GRAM + BASIS * BASIS)
    weight = jnp.where(inside, jnp.where(gi == gj, 1.0, 2.0), 0.0)
    terms = left * right * tile * weight
    terms = terms + jnp.where(lane == BASIS, tile, 0.0)
    terms = terms - jnp.where(lane < BASIS, 2.0 * tile * tile, 0.0)
    squares = jnp.maximum(jnp.sum(terms, axis=1, keepdims=True), 0.0)
    norm = jnp.sqrt(squares + 1e-06)
    inv_norm = 1.0 / norm
    coef_ref[...] = jnp.where(lane == BASIS, norm, tile)

    outs = []
    for part, dst in enumerate((og_hbm, ou_hbm, od_hbm)):

        def final(i, carry, part=part):
            cols = pl.ds(pl.multiple_of(i * 256, 256), 256)
            left_over = w_v[part, :, cols]
            for j in range(BASIS):
                left_over = left_over - proj[j] * k_v[part, j, :, cols].astype(F32)
            out_v[part, :, cols] = (left_over * inv_norm).astype(BF16)
            return carry

        lax.fori_loop(0, D // 256, final, 0)
        cp = pltpu.make_async_copy(out_v.at[part], dst, osem.at[part])
        cp.start()
        outs.append(cp)
    for cp in pending:
        cp.wait_send()
    for cp in outs:
        cp.wait()


def per_device(
    inputs, norm_gain, lengths, gate_rows, up_rows, down_rows, krylov_gate, krylov_up, krylov_down
):
    devices = lax.axis_size("fsdp")
    Z, A = sides(devices)
    D = inputs.shape[1]
    T = inputs.shape[0] * devices
    L = T * 3 // 4
    BASIS, F, _ = krylov_gate.shape
    R = D // 128
    H = D // 2
    W = H // A
    cfg = (Z, A, D, T, L, F, BASIS)
    pairs = BASIS * (BASIS + 1) // 2
    n1 = Z - 1 + 2 * (A - 1) + A
    n2 = A + 2 * (A - 1) + Z - 1
    n3 = Z - 1 + A - 1 + A * (A - 1) + A * A + 1 + 2 * (A - 1) + Z - 1
    hbm = pl.BlockSpec(memory_space=pl.ANY)
    part = jax.ShapeDtypeStruct((F, D), BF16)
    dma = pltpu.SemaphoreType.DMA
    out = pl.pallas_call(
        functools.partial(body, cfg),
        out_shape=(part, part, part, jax.ShapeDtypeStruct((1, 128), F32)),
        in_specs=[pl.BlockSpec(memory_space=pltpu.SMEM)] + [hbm] * 8,
        out_specs=(hbm, hbm, hbm, pl.BlockSpec(memory_space=pltpu.VMEM)),
        scratch_shapes=[
            pltpu.VMEM((R, 128), BF16),
            pltpu.VMEM((R, 128), BF16),
            pltpu.VMEM((F, D), BF16),
            pltpu.VMEM((F, D), BF16),
            pltpu.VMEM((F, D), BF16),
            pltpu.VMEM((3, BASIS, F, D), BF16),
            pltpu.VMEM((Z, A, R, 128), BF16),
            pltpu.VMEM((Z * A * R, 128), F32),
            pltpu.VMEM((2, A, Z * A, D), BF16),
            pltpu.VMEM((4 * F, D), BF16),
            pltpu.VMEM((L, T), BF16),
            pltpu.VMEM((L, D), BF16),
            pltpu.VMEM((4 * F, L), F32),
            pltpu.VMEM((A, L, W), BF16),
            pltpu.VMEM((A, L, W), BF16),
            pltpu.VMEM((A, L, W), F32),
            pltpu.VMEM((A - 1, L, W), BF16),
            pltpu.VMEM((A - 1, L, W), BF16),
            pltpu.VMEM((A - 1, L, 128), BF16),
            pltpu.VMEM((A - 1, L, 128), BF16),
            pltpu.VMEM((L, 128), F32),
            pltpu.VMEM((Z - 1, L // Z, 128), F32),
            pltpu.VMEM((L, 128), F32),
            pltpu.VMEM((L, D), BF16),
            pltpu.VMEM((F, L), F32),
            pltpu.VMEM((3, F, D), F32),
            pltpu.VMEM((pairs, 8, 128), F32),
            pltpu.VMEM((128, 128), F32),
            pltpu.VMEM((2, 8, 128), F32),
            pltpu.VMEM((A, 8, 128), F32),
            pltpu.VMEM((A, 8, 128), F32),
            pltpu.VMEM((Z, 8, 128), F32),
            pltpu.VMEM((8, 128), F32),
            pltpu.VMEM((3, F, D), BF16),
            dma((5,)),
            dma((3,)),
            dma((3,)),
            dma((n1,)),
            dma((n1,)),
            dma((n2,)),
            dma((n2,)),
            dma((n3,)),
            dma((n3,)),
        ],
        compiler_params=pltpu.CompilerParams(
            collective_id=0, has_side_effects=True, vmem_limit_bytes=60 << 20
        ),
        name="arnoldi_step",
    )(
        lengths,
        inputs.reshape(R, 128),
        norm_gain.reshape(R, 128),
        gate_rows,
        up_rows,
        down_rows,
        krylov_gate,
        krylov_up,
        krylov_down,
    )
    return (out[0], out[1], out[2], out[3][0, : BASIS + 1])


def solution(mesh):
    placed = (
        P("fsdp", None),
        P(),
        P(),
        P("fsdp", None),
        P("fsdp", None),
        P("fsdp", None),
        P(None, "fsdp", None),
        P(None, "fsdp", None),
        P(None, "fsdp", None),
    )
    return jax.shard_map(
        per_device,
        mesh=mesh,
        in_specs=placed,
        out_specs=(P("fsdp", None), P("fsdp", None), P("fsdp", None), P()),
        check_vma=False,
    )
```

time: 1770 us -> 101 us (0.06)
  the two profiles are of different devices: /device:TPU:1 before, /device:TPU:16 now
where the time goes in v1:
time: 101 us
  Pallas kernels  92.5 us (92%)
  local copies, waits for them, and re-layouts  6.33 us (6%)
  other arithmetic  1.37 us (1%)
    pallas_call x1, Pallas kernels, per_device(): pl.pallas_call(functools.partial(body, cfg), out_shape=(part, part, part,...  92.5 us
    unnamed x3, local copies, waits for them, and re-layouts  5.15 us

profile of v1, /device:TPU:16, one launch (start us, length us, event | category | flops | bytes accessed | tf_op | source)
XLA Modules:
  0.0 100.8 jit_solution(17278404011923391046)
XLA Ops:
  0.6 1.4 %reduce = bf16[4096]{0:T(1024)(128)(2,1)} reduce(bf16[1,4096]{1,0:T(2,128)(2,1)} %param.9, bf16[]{:T(256)} %constant.7), dimensions={0}, to_apply=%param.9.reduce_sub_computation | reduce | bytes 16386 | tf_op args[0]
  2.0 92.5 %arnoldi_step.1 = (bf16[40,4096]{1,0:T(8,128)(2,1)}, bf16[40,4096]{1,0:T(8,128)(2,1)}, bf16[40,4096]{1,0:T(8,128)(2,1)}, f32[1,128]{1,0:T(1,128)}) custom-call(s32[2]{0:T(128)} %len_ref.1, bf16[32,128]{1,0:T(8,128)(2,1)} %bitcast.4, bf16[32,128]{1,0:T(8,128)(2,1)} %bitcast.5, bf16[40,4096]{1,0:T(8,128)(2,1)} %gate_hbm.1, bf16[40,4096]{1,0:T(8,128)(2,1)} %up_hbm.1, ...), custom_call_target="tpu_custom_call" | custom-call | tf_op jit(solution)/shard_map/arnoldi_step/pallas_call | solution.py:520
  94.5 1.2 %slice_bitcast_fusion = f32[9]{0:T(128)} fusion(f32[1,128]{1,0:T(1,128)} %get-tuple-element.11), kind=kLoop, calls=%fused_computation | loop fusion | bytes 72 | tf_op jit(solution)/shard_map/squeeze | solution.py:585
  95.7 1.7 %copy.16 = bf16[40,4096]{1,0:T(8,128)(2,1)} copy(bf16[40,4096]{1,0:T(8,128)(2,1)} %get-tuple-element.16) | data formatting | bytes 655360
  97.4 1.7 %copy.17 = bf16[40,4096]{1,0:T(8,128)(2,1)} copy(bf16[40,4096]{1,0:T(8,128)(2,1)} %get-tuple-element.17) | data formatting | bytes 655360
  99.1 1.7 %copy.18 = bf16[40,4096]{1,0:T(8,128)(2,1)} copy(bf16[40,4096]{1,0:T(8,128)(2,1)} %get-tuple-element.18) | data formatting | bytes 655360

commit v2 on v1

v2 whole, which is shorter than its diff:
```python
import functools
import math

import jax
import jax.numpy as jnp
from jax import lax
from jax.experimental import pallas as pl
from jax.experimental.pallas import tpu as pltpu
from jax.sharding import PartitionSpec as P

MESH = pl.DeviceIdType.MESH
F32 = jnp.float32
BF16 = jnp.bfloat16
GRAM = 16


def sides(devices):
    return {256: (8, 4), 16: (2, 2)}[devices]


def gelu_pair(gate_pre):
    coef = math.sqrt(2.0 / math.pi)
    cube = gate_pre * gate_pre * gate_pre
    tanh_val = jnp.tanh(coef * (gate_pre + 0.044715 * cube))
    act = 0.5 * gate_pre * (1.0 + tanh_val)
    slope = 0.5 * (1.0 + tanh_val) + 0.5 * gate_pre * (1.0 - tanh_val * tanh_val) * coef * (
        1.0 + 3.0 * 0.044715 * gate_pre * gate_pre
    )
    return (act, slope)


def mm(left, right):
    return jnp.dot(left, right, preferred_element_type=F32)


def mm_last(left, right):
    return lax.dot_general(left, right, (((1,), (1,)), ((), ())), preferred_element_type=F32)


def fold(value):
    rows = value.shape[0]
    total = value[0:8]
    for start in range(8, rows, 8):
        total = total + value[start : start + 8]
    return total


def near_first(count):
    return {8: (0, 1, 7, 2, 6, 3, 5, 4), 2: (0, 1)}[count]


def body(
    cfg,
    len_ref,
    x_hbm,
    gain_hbm,
    gate_hbm,
    up_hbm,
    down_hbm,
    kg_hbm,
    ku_hbm,
    kd_hbm,
    w_v,
    k_v,
    coef_ref,
    x_v,
    gain_v,
    gate_v,
    up_v,
    down_v,
    x32,
    rowbuf,
    rows32,
    tok,
    w4,
    sel,
    nc,
    every,
    pre,
    psend,
    precv,
    own,
    asend,
    arecv,
    bsend,
    brecv,
    zsum,
    zrecv,
    lz,
    loss,
    backacc,
    gacc,
    qrows,
    sc_zc,
    sc_xy,
    lsem,
    ksem,
    s1,
    r1,
    s2,
    r2,
    s3,
    r3,
    s4,
    r4,
):
    Z, A, D, T, L, F, BASIS = cfg
    H = D // 2
    W = H // A
    RZ = L // Z
    R = D // 128
    CH = min(512, D)
    LEN = T // 2
    HZ = Z // 2
    HL = L // 2
    NEAR = near_first(Z)
    SLOT = {k: g for g, k in enumerate(NEAR)}
    inv_d = 1.0 / math.sqrt(D)
    inv_ff = 1.0 / math.sqrt(F * T)
    inv_count = 1.0 / (3.0 * D * F * T)
    plane = 2 * A * A

    me = lax.axis_index("fsdp")
    c = lax.rem(me, 2)
    y = lax.rem(me // 2, A)
    x = lax.rem(me // (2 * A), A)
    z = me // plane
    sa = 2 * A - (2 * A - 2) * c
    sb = 2 + (2 * A - 2) * c
    a = x + c * (y - x)
    b = y + c * (x - y)
    partner = me + 1 - 2 * c

    def step(i, k, n):
        return lax.rem(i + k, n)

    def back_of(i, k, n):
        return lax.rem(i + n - k, n)

    def dev_z(k):
        return me + (step(z, k, Z) - z) * plane

    def dev_a(k):
        return me + (step(a, k, A) - a) * sa

    def dev_b(k):
        return me + (step(b, k, A) - b) * sb

    def dev_zc(k, flip):
        return dev_z(k) + flip * (1 - 2 * c)

    def dev_xy(kx, ky):
        return me + (step(x, kx, A) - x) * (2 * A) + (step(y, ky, A) - y) * 2

    pending = []

    def send(src, dst, ss, rs, dev):
        cp = pltpu.make_async_remote_copy(
            src_ref=src, dst_ref=dst, send_sem=ss, recv_sem=rs, device_id=(dev,), device_id_type=MESH
        )
        cp.start()
        pending.append(cp)
        return cp

    zc_group = [(k, flip) for k in range(Z) for flip in range(2) if k or flip]
    xy_group = [(kx, ky) for kx in range(A) for ky in range(A) if kx or ky]
    barrier = pltpu.get_barrier_semaphore()
    peers = [dev_zc(k, flip) for k, flip in zc_group] + [dev_xy(kx, ky) for kx, ky in xy_group]
    for peer in peers:
        pl.semaphore_signal(barrier, inc=1, device_id=(peer,), device_id_type=MESH)

    loads = []
    for i, (src, dst) in enumerate(
        ((x_hbm, x_v), (gain_hbm, gain_v), (gate_hbm, gate_v), (up_hbm, up_v), (down_hbm, down_v))
    ):
        cp = pltpu.make_async_copy(src, dst, lsem.at[i])
        cp.start()
        loads.append(cp)
    kloads = []
    for i, src in enumerate((kg_hbm, ku_hbm, kd_hbm)):
        cp = pltpu.make_async_copy(src, k_v.at[i], ksem.at[i])
        cp.start()
        kloads.append(cp)

    loads[0].wait()
    loads[1].wait()
    flat = x_v[...].astype(F32)
    for d in range(R):
        x32[d : d + 1, :] = flat[:, d * 128 : (d + 1) * 128]
    wide = x32[...]
    square = jnp.sum(jnp.sum(wide * wide, axis=1, keepdims=True), axis=0, keepdims=True)
    normed_own = wide * lax.rsqrt(square * (1.0 / D) + 1e-06) * gain_v[...].astype(F32)
    rowbuf[0, a] = normed_own.astype(BF16)

    gacc[...] = jnp.zeros_like(gacc)

    def gram(part):
        def chunk(i, carry):
            cols = pl.ds(pl.multiple_of(i * 128, 128), 128)
            ks = [k_v[part, j, :, cols].astype(F32) for j in range(BASIS)]
            n = 0
            for i1 in range(BASIS):
                for j1 in range(i1, BASIS):
                    gacc[n] += fold(ks[i1] * ks[j1])
                    n += 1
            return carry

        lax.fori_loop(0, D // 128, chunk, 0)

    pl.semaphore_wait(barrier, len(peers))

    zcps = {}
    for k in NEAR[1:]:
        g = SLOT[Z - k]
        zcps[g] = send(rowbuf.at[0, a], rowbuf.at[g, a], s1.at[g], r1.at[g], dev_z(k))
    o = Z

    def sem1(group, n):
        return o + group * n

    base = Z
    acps = [None, None]
    for h in range(2):
        for g in range(max(1, h * HZ), (h + 1) * HZ):
            zcps[g].wait_recv()
        mine = rowbuf.at[pl.ds(h * HZ, HZ), a]
        acps[h] = []
        for k in range(1, A):
            n = base + h * (A - 1) + k - 1
            acps[h].append(send(mine, mine, s1.at[n], r1.at[n], dev_a(k)))
        if h == 0:
            kloads[0].wait()
    base += 2 * (A - 1)
    bcps = [None, None]
    pcps = [[], []]
    pbase = base + 2 * (A - 1)
    for h in range(2):
        for cp in acps[h]:
            cp.wait_recv()
        for i in range(HZ):
            for j in range(A):
                rows32[pl.ds((i * A + j) * R, R), :] = rowbuf[h * HZ + i, j].astype(F32)
        for d in range(R):
            tok[h, c, b, :, pl.ds(d * 128, 128)] = rows32[pl.ds(d, HZ * A, stride=R), :].astype(BF16)
        mine = tok.at[h, c, b]
        bcps[h] = []
        for k in range(1, A):
            n = base + h * (A - 1) + k - 1
            bcps[h].append(send(mine, mine, s1.at[n], r1.at[n], dev_b(k)))
        n = pbase + h * A
        pcps[h].append(send(mine, mine, s1.at[n], r1.at[n], partner))
    gram(0)
    kloads[1].wait()
    loads[2].wait()
    loads[3].wait()
    loads[4].wait()

    def stack(i, carry):
        cols = pl.ds(pl.multiple_of(i * CH, CH), CH)
        parts = [gate_v[:, cols], up_v[:, cols], k_v[0, BASIS - 1, :, cols], k_v[1, BASIS - 1, :, cols]]
        w4[:, cols] = jnp.concatenate([p.astype(F32) for p in parts], axis=0).astype(BF16)
        return carry

    lax.fori_loop(0, D // CH, stack, 0)
    len0 = len_ref[0]
    len1 = len_ref[1]
    col = lax.broadcasted_iota(jnp.int32, (L, T), 1)
    row = lax.broadcasted_iota(jnp.int32, (L, T), 0)

    def offset(g):
        k = jnp.zeros_like(g)
        for slot in range(1, Z):
            k = jnp.where(g == slot, NEAR[slot], k)
        return lax.rem(k + z, Z)

    gh = col // (T // 2)
    gc = lax.rem(col // (T // 4), 2)
    gb = lax.rem(col // (HZ * A), A)
    gz = offset(gh * HZ + lax.rem(col // A, HZ))
    ga = lax.rem(col, A)
    gx = ga + gc * (gb - ga)
    gy = gb + gc * (ga - gb)
    token = gz * plane + gx * (2 * A) + gy * 2 + gc
    second = token >= LEN
    inner = jnp.where(second, token - LEN, token)
    live = inner < jnp.where(second, len1, len0)
    place = jnp.where(live, inner + jnp.where(second, len0, 0), -1)
    wanted = offset(row // RZ) * RZ + lax.rem(row, RZ)
    sel[...] = jnp.where(place == wanted, 1.0, 0.0).astype(BF16)
    for h in range(2):
        for k in range(1, A):
            bcps[h][k - 1].wait_recv()
            ref = tok.at[h, c, back_of(b, k, A)]
            n = pbase + h * A + k
            pcps[h].append(send(ref, ref, s1.at[n], r1.at[n], partner))
        if h == 0:
            gram(1)

    every[...] = jnp.zeros_like(every)
    for h in range(2):
        for cp in pcps[h]:
            cp.wait_recv()

        def first(i, carry, h=h):
            cols = pl.ds(pl.multiple_of(i * CH, CH), CH)
            half = tok[h, :, :, :, cols].reshape(T // 2, CH)
            every[h] += mm_last(w4[:, cols], half)
            return carry

        lax.fori_loop(0, D // CH, first, 0)
    whole = jnp.concatenate([every[0], every[1]], axis=1)
    moved = None
    for _ in range(3):
        term = whole.astype(BF16)
        whole = whole - term.astype(F32)
        term = mm_last(term, sel[...])
        moved = term if moved is None else moved + term
    pre[...] = moved
    gate_pre = pre[0:F]
    up_pre = pre[F : 2 * F]
    tan_gate = pre[2 * F : 3 * F] * inv_d
    tan_up = pre[3 * F : 4 * F] * inv_d
    act, slope = gelu_pair(gate_pre)
    hidden = act * up_pre
    tangent = slope * tan_gate * up_pre + act * tan_up
    hid_t = hidden.T.astype(BF16)
    tan_t = tangent.T.astype(BF16)
    kloads[2].wait()

    def jvp_block(start):
        cols = pl.ds(pl.multiple_of(start, 128), W)
        return mm(tan_t, down_v[:, cols]) + mm(hid_t, k_v[2, BASIS - 1, :, cols]) * inv_ff

    order = list(range(1, A)) + [0]
    pcps = [None] * A
    for k in order:
        psend[k] = jvp_block((1 - c) * H + step(b, k, A) * W).astype(BF16)
        pcps[k] = send(psend.at[k], precv.at[k], s2.at[k], r2.at[k], partner)
    base = A
    halves = (1, 0)
    acps = [[], []]

    def pass_a(h, k, total):
        if k:
            n = base + h * (A - 1) + k - 1
            asend[h, k - 1] = total.astype(BF16)
            acps[h].append(send(asend.at[h, k - 1], arecv.at[h, k - 1], s2.at[n], r2.at[n], dev_a(k)))
        else:
            own[0, h * HL : (h + 1) * HL, :] = total

    for k in order:
        mine = jvp_block(c * H + step(a, k, A) * W)
        pcps[k].wait_recv()
        total = mine + precv[k].astype(F32)
        own[k] = total
        pass_a(1, k, total[HL:L])
    for k in order:
        pass_a(0, k, own[k, 0:HL, :])
    gram(2)
    base += 2 * (A - 1)
    bcps = [[], []]
    for h in halves:
        rows = slice(h * HL, (h + 1) * HL)
        for cp in acps[h]:
            cp.wait_recv()
        for k in order:
            cols = pl.ds(pl.multiple_of(step(b, k, A) * 128, 128), 128)
            total = own[0, rows, cols]
            for j in range(A - 1):
                total = total + arecv[h, j, :, cols].astype(F32)
            if k:
                n = base + h * (A - 1) + k - 1
                bsend[h, k - 1] = total.astype(BF16)
                bcps[h].append(send(bsend.at[h, k - 1], brecv.at[h, k - 1], s2.at[n], r2.at[n], dev_b(k)))
            else:
                zsum[rows, :] = total
    base += 2 * (A - 1)
    zcps = []
    for h in halves:
        rows = slice(h * HL, (h + 1) * HL)
        for cp in bcps[h]:
            cp.wait_recv()
        total = zsum[rows, :]
        for j in range(A - 1):
            total = total + brecv[h, j].astype(F32)
        zsum[rows, :] = total
        for g in range(max(1, h * HZ), (h + 1) * HZ):
            k = NEAR[g]
            zcps.append(
                send(zsum.at[pl.ds(g * RZ, RZ)], zrecv.at[k - 1], s2.at[base + k], r2.at[base + k], dev_z(k))
            )
    def keep(i, carry):
        cols = pl.ds(pl.multiple_of(i * CH, CH), CH)
        nc[:, cols] = mm(sel[...], tok[:, :, :, :, cols].reshape(T, CH)).astype(BF16)
        return carry

    lax.fori_loop(0, D // CH, keep, 0)
    for cp in zcps:
        cp.wait_recv()
    total = zsum[0:RZ, :]
    for j in range(Z - 1):
        total = total + zrecv[j]
    lz[0] = total.astype(BF16)

    zcps = {}
    for k in NEAR[1:]:
        g = SLOT[Z - k]
        zcps[g] = send(lz.at[0], lz.at[g], s3.at[g], r3.at[g], dev_z(k))
    base = Z
    abase = base + 2 * (A - 1)
    pbase = abase + 2 * A * (A - 1)
    bcps = [[], []]
    acps = {}
    pcps = []

    def pass_on(h, kb):
        ref = loss.at[h, c, a, back_of(b, kb, A)]
        for k in range(1, A):
            n = abase + (h * A + kb) * (A - 1) + k - 1
            acps[h, kb, k] = send(ref, ref, s3.at[n], r3.at[n], dev_a(k))
        n = pbase + h * (2 * A - 1) + kb
        pcps.append(send(ref, ref, s3.at[n], r3.at[n], partner))

    for h in range(2):
        for g in range(max(1, h * HZ), (h + 1) * HZ):
            zcps[g].wait_recv()
        groups = [lz[g].astype(F32) for g in range(h * HZ, (h + 1) * HZ)]
        mine = groups[0] if len(groups) == 1 else jnp.concatenate(groups, axis=0)
        loss[h, c, a, b] = mine.astype(BF16)
        ref = loss.at[h, c, a, b]
        for k in range(1, A):
            n = base + h * (A - 1) + k - 1
            bcps[h].append(send(ref, ref, s3.at[n], r3.at[n], dev_b(k)))
        pass_on(h, 0)
    for h in range(2):
        for kb in range(1, A):
            bcps[h][kb - 1].wait_recv()
            pass_on(h, kb)
    for h in range(2):
        for k in range(1, A):
            for kb in range(A):
                acps[h, kb, k].wait_recv()
            ref = loss.at[h, c, back_of(a, k, A)]
            n = pbase + h * (2 * A - 1) + A + k - 1
            pcps.append(send(ref, ref, s3.at[n], r3.at[n], partner))
    backacc[...] = jnp.zeros_like(backacc)
    PER = CH // 128

    def loss_cols(i):
        halves = []
        for h in range(2):
            blocks = []
            for j in range(PER):
                n = i * PER + j
                blocks.append(loss[h, n // (A * A), lax.rem(n // A, A), lax.rem(n, A)])
            halves.append(jnp.concatenate(blocks, axis=1))
        return jnp.concatenate(halves, axis=0)

    def second_pass(i, carry):
        cols = pl.ds(pl.multiple_of(i * CH, CH), CH)
        backacc[...] += mm_last(down_v[:, cols], loss_cols(i))
        return carry

    count = D // CH // 2
    lax.fori_loop(c * count, c * count + count, second_pass, 0)
    for cp in pcps:
        cp.wait_recv()
    lax.fori_loop((1 - c) * count, (1 - c) * count + count, second_pass, 0)
    back = backacc[...]
    gate_pre = pre[0:F]
    up_pre = pre[F : 2 * F]
    act, slope = gelu_pair(gate_pre)
    hid = (act * up_pre).astype(BF16)
    both = jnp.concatenate([back * up_pre * slope, back * act], axis=0).astype(BF16)

    def grads(i, carry):
        cols = pl.ds(pl.multiple_of(i * CH, CH), CH)
        two = mm(both, nc[:, cols]) * inv_d
        three = mm(hid, loss_cols(i)) * inv_ff
        parts = (two[0:F], two[F : 2 * F], three)
        carry = list(carry)
        for part in range(3):
            grad = parts[part]
            w_v[part, :, cols] = grad
            for sub in range(CH // 128):
                g = grad[:, sub * 128 : (sub + 1) * 128]
                scols = pl.ds(pl.multiple_of(i * CH + sub * 128, 128), 128)
                for j in range(BASIS):
                    carry[j] = carry[j] + fold(k_v[part, j, :, scols].astype(F32) * g)
                carry[BASIS] = carry[BASIS] + fold(g * g)
        return tuple(carry)

    zero = jnp.zeros((8, 128), F32)
    sums = lax.fori_loop(0, D // CH, grads, (zero,) * (BASIS + 1))
    qrows[...] = jnp.zeros_like(qrows)
    for j in range(BASIS + 1):
        qrows[j : j + 1, :] = jnp.sum(sums[j], axis=0, keepdims=True)
    n = 0
    for i1 in range(BASIS):
        for j1 in range(i1, BASIS):
            q = GRAM + i1 * BASIS + j1
            qrows[q : q + 1, :] = jnp.sum(gacc[n], axis=0, keepdims=True)
            n += 1
    line = jnp.sum(qrows[...], axis=1, keepdims=True) * inv_count
    rowi = lax.broadcasted_iota(jnp.int32, (128, 128), 0)
    coli = lax.broadcasted_iota(jnp.int32, (128, 128), 1)
    tile = jnp.sum(jnp.where(rowi == coli, line, 0.0), axis=0, keepdims=True)

    def share(slots, value, at, devs, base):
        slots[at] = value
        cps = []
        for n, dev in enumerate(devs):
            cps.append(send(slots.at[at], slots.at[at], s4.at[base + n], r4.at[base + n], dev))
        for cp in cps:
            cp.wait_recv()
        total = slots[0]
        for j in range(1, len(devs) + 1):
            total = total + slots[j]
        return total

    tile = share(sc_zc, tile, z * 2 + c, [dev_zc(k, flip) for k, flip in zc_group], 0)
    tile = share(sc_xy, tile, x * A + y, [dev_xy(kx, ky) for kx, ky in xy_group], len(zc_group))
    coef_ref[...] = tile
    for cp in pending:
        cp.wait_send()


def finish(cfg, coef_in, w_v, k_v, og_hbm, ou_hbm, od_hbm, coef_ref, out_v, osem):
    D, F, BASIS = cfg
    tile = coef_in[...]
    lane = lax.broadcasted_iota(jnp.int32, (1, 128), 1)
    proj = [
        jnp.sum(jnp.where(lane == j, tile, 0.0), axis=1, keepdims=True) for j in range(BASIS)
    ]
    gi = (lane - GRAM) // BASIS
    gj = lax.rem(lane + (8 * BASIS - GRAM), BASIS)
    left = jnp.zeros_like(tile)
    right = jnp.zeros_like(tile)
    for j in range(BASIS):
        left = left + jnp.where(gi == j, proj[j], 0.0)
        right = right + jnp.where(gj == j, proj[j], 0.0)
    inside = (lane >= GRAM) & (lane < GRAM + BASIS * BASIS)
    weight = jnp.where(inside, jnp.where(gi == gj, 1.0, 2.0), 0.0)
    terms = left * right * tile * weight
    terms = terms + jnp.where(lane == BASIS, tile, 0.0)
    terms = terms - jnp.where(lane < BASIS, 2.0 * tile * tile, 0.0)
    squares = jnp.maximum(jnp.sum(terms, axis=1, keepdims=True), 0.0)
    norm = jnp.sqrt(squares + 1e-06)
    inv_norm = 1.0 / norm
    for j in range(BASIS):
        coef_ref[j] = jnp.sum(jnp.where(lane == j, tile, 0.0))
    coef_ref[BASIS] = jnp.sum(jnp.where(lane == 0, norm, 0.0))

    outs = []
    for part, dst in enumerate((og_hbm, ou_hbm, od_hbm)):

        def final(i, carry, part=part):
            cols = pl.ds(pl.multiple_of(i * 256, 256), 256)
            left_over = w_v[part, :, cols]
            for j in range(BASIS):
                left_over = left_over - proj[j] * k_v[part, j, :, cols].astype(F32)
            out_v[part, :, cols] = (left_over * inv_norm).astype(BF16)
            return carry

        lax.fori_loop(0, D // 256, final, 0)
        cp = pltpu.make_async_copy(out_v.at[part], dst, osem.at[part])
        cp.start()
        outs.append(cp)
    for cp in outs:
        cp.wait()


def per_device(
    inputs, norm_gain, lengths, gate_rows, up_rows, down_rows, krylov_gate, krylov_up, krylov_down
):
    devices = lax.axis_size("fsdp")
    Z, A = sides(devices)
    D = inputs.shape[1]
    T = inputs.shape[0] * devices
    L = T * 3 // 4
    BASIS, F, _ = krylov_gate.shape
    R = D // 128
    H = D // 2
    W = H // A
    HZ = Z // 2
    HL = L // 2
    cfg = (Z, A, D, T, L, F, BASIS)
    pairs = BASIS * (BASIS + 1) // 2
    n1 = Z + 4 * (A - 1) + 2 * A
    n2 = A + 4 * (A - 1) + Z
    n3 = Z + 2 * (A - 1) + 2 * A * (A - 1) + 2 * (2 * A - 1)
    n4 = 2 * Z - 1 + A * A - 1
    hbm = pl.BlockSpec(memory_space=pltpu.HBM)
    vmem = pl.BlockSpec(memory_space=pltpu.VMEM)
    dma = pltpu.SemaphoreType.DMA
    w, k, sums = pl.pallas_call(
        functools.partial(body, cfg),
        out_shape=(
            pltpu.VMEM((3, F, D), F32),
            pltpu.VMEM((3, BASIS, F, D), BF16),
            pltpu.VMEM((1, 128), F32),
        ),
        in_specs=[pl.BlockSpec(memory_space=pltpu.SMEM)] + [hbm] * 8,
        out_specs=(vmem, vmem, vmem),
        scratch_shapes=[
            pltpu.VMEM((1, D), BF16),
            pltpu.VMEM((R, 128), BF16),
            pltpu.VMEM((F, D), BF16),
            pltpu.VMEM((F, D), BF16),
            pltpu.VMEM((F, D), BF16),
            pltpu.VMEM((R, 128), F32),
            pltpu.VMEM((Z, A, R, 128), BF16),
            pltpu.VMEM((HZ * A * R, 128), F32),
            pltpu.VMEM((2, 2, A, HZ * A, D), BF16),
            pltpu.VMEM((4 * F, D), BF16),
            pltpu.VMEM((L, T), BF16),
            pltpu.VMEM((L, D), BF16),
            pltpu.VMEM((2, 4 * F, T // 2), F32),
            pltpu.VMEM((4 * F, L), F32),
            pltpu.VMEM((A, L, W), BF16),
            pltpu.VMEM((A, L, W), BF16),
            pltpu.VMEM((A, L, W), F32),
            pltpu.VMEM((2, A - 1, HL, W), BF16),
            pltpu.VMEM((2, A - 1, HL, W), BF16),
            pltpu.VMEM((2, A - 1, HL, 128), BF16),
            pltpu.VMEM((2, A - 1, HL, 128), BF16),
            pltpu.VMEM((L, 128), F32),
            pltpu.VMEM((Z - 1, L // Z, 128), F32),
            pltpu.VMEM((Z, L // Z, 128), BF16),
            pltpu.VMEM((2, 2, A, A, HL, 128), BF16),
            pltpu.VMEM((F, L), F32),
            pltpu.VMEM((pairs, 8, 128), F32),
            pltpu.VMEM((128, 128), F32),
            pltpu.VMEM((2 * Z, 1, 128), F32),
            pltpu.VMEM((A * A, 1, 128), F32),
            dma((5,)),
            dma((3,)),
            dma((n1,)),
            dma((n1,)),
            dma((n2,)),
            dma((n2,)),
            dma((n3,)),
            dma((n3,)),
            dma((n4,)),
            dma((n4,)),
        ],
        compiler_params=pltpu.CompilerParams(
            collective_id=0, has_side_effects=True, vmem_limit_bytes=57200000
        ),
        name="arnoldi_step",
    )(
        lengths,
        inputs,
        norm_gain.reshape(R, 128),
        gate_rows,
        up_rows,
        down_rows,
        krylov_gate,
        krylov_up,
        krylov_down,
    )
    part = jax.ShapeDtypeStruct((F, D), BF16)
    return pl.pallas_call(
        functools.partial(finish, (D, F, BASIS)),
        out_shape=(part, part, part, jax.ShapeDtypeStruct((BASIS + 1,), F32)),
        in_specs=[vmem, vmem, vmem],
        out_specs=(hbm, hbm, hbm, pl.BlockSpec(memory_space=pltpu.SMEM)),
        scratch_shapes=[pltpu.VMEM((3, F, D), BF16), dma((3,))],
        compiler_params=pltpu.CompilerParams(vmem_limit_bytes=8 << 20),
        name="arnoldi_finish",
    )(sums, w, k)


def solution(mesh):
    placed = (
        P("fsdp", None),
        P(),
        P(),
        P("fsdp", None),
        P("fsdp", None),
        P("fsdp", None),
        P(None, "fsdp", None),
        P(None, "fsdp", None),
        P(None, "fsdp", None),
    )
    return jax.shard_map(
        per_device,
        mesh=mesh,
        in_specs=placed,
        out_specs=(P("fsdp", None), P("fsdp", None), P("fsdp", None), P()),
        check_vma=False,
    )
```

time: 101 us -> 83.2 us (0.82)
  the two profiles are of different devices: /device:TPU:16 before, /device:TPU:1 now
where the time goes in v2:
time: 83.2 us; the launch traced here: 83.1 us
  Pallas kernels  82.4 us (99%)
    pallas_call x1, Pallas kernels, per_device(): pl.pallas_call(functools.partial(body, cfg), out_shape=(pltpu.VMEM((3, F,...  78.9 us
    pallas_call x1, Pallas kernels, per_device(): pl.pallas_call(functools.partial(finish, (D, F, BASIS)), out_shape=(part,...  3.53 us

profile of v2, /device:TPU:1, one launch (start us, length us, event | category | flops | bytes accessed | tf_op | source)
XLA Modules:
  0.0 83.1 jit_solution(11093815312744647705)
XLA Ops:
  0.6 78.9 %arnoldi_step.1 = (f32[3,40,4096]{2,1,0:T(8,128)S(1)}, bf16[3,8,40,4096]{3,2,1,0:T(8,128)(2,1)S(1)}, f32[1,128]{1,0:T(1,128)S(1)}) custom-call(s32[2]{0:T(128)} %len_ref.1, bf16[1,4096]{1,0:T(2,128)(2,1)} %x_hbm.1, bf16[32,128]{1,0:T(8,128)(2,1)} %bitcast.1, bf16[40,4096]{1,0:T(8,128)(2,1)} %gate_hbm.1, bf16[40,4096]{1,0:T(8,128)(2,1)} %up_hbm.1, ...), custom_call_target="tpu_custom_call" | custom-call | tf_op jit(solution)/shard_map/arnoldi_step/pallas_call | solution.py:596
  79.5 3.5 %arnoldi_finish.1 = (bf16[40,4096]{1,0:T(8,128)(2,1)}, bf16[40,4096]{1,0:T(8,128)(2,1)}, bf16[40,4096]{1,0:T(8,128)(2,1)}, f32[9]{0:T(128)}) custom-call(f32[1,128]{1,0:T(1,128)S(1)} %get-tuple-element.7.coef_in, f32[3,40,4096]{2,1,0:T(8,128)S(1)} %get-tuple-element.8.w_v, bf16[3,8,40,4096]{3,2,1,0:T(8,128)(2,1)S(1)} %get-tuple-element.9.k_v), custom_call_target="tpu_custom_call" | custom-call | tf_op jit(solution)/shard_map/arnoldi_finish/pallas_call | solution.py:663

commit v3 on v2

--- a/solution.py
+++ b/solution.py
@@ -72,7 +72,8 @@
     rowbuf,
     rows32,
     tok,
-    w4,
+    w4t,
+    downt,
     sel,
     nc,
     every,
@@ -85,12 +86,17 @@
     bsend,
     brecv,
     zsum,
+    zsend,
     zrecv,
     lz,
     loss,
     backacc,
     gacc,
     qrows,
+    drows,
+    act_v,
+    bend_v,
+    hid_v,
     sc_zc,
     sc_xy,
     lsem,
@@ -110,10 +116,13 @@
     RZ = L // Z
     R = D // 128
     CH = min(512, D)
+    CW = min(1024, D // 2)
     LEN = T // 2
     HZ = Z // 2
     HL = L // 2
     NEAR = near_first(Z)
+    NS = min(2, Z)
+    G = Z // NS
     SLOT = {k: g for g, k in enumerate(NEAR)}
     inv_d = 1.0 / math.sqrt(D)
     inv_ff = 1.0 / math.sqrt(F * T)
@@ -194,7 +203,7 @@
 
     gacc[...] = jnp.zeros_like(gacc)
 
-    def gram(part):
+    def gram(part, low, high):
         def chunk(i, carry):
             cols = pl.ds(pl.multiple_of(i * 128, 128), 128)
             ks = [k_v[part, j, :, cols].astype(F32) for j in range(BASIS)]
@@ -205,7 +214,7 @@
                     n += 1
             return carry
 
-        lax.fori_loop(0, D // 128, chunk, 0)
+        lax.fori_loop(low, high, chunk, 0)
 
     pl.semaphore_wait(barrier, len(peers))
 
@@ -230,6 +239,7 @@
             acps[h].append(send(mine, mine, s1.at[n], r1.at[n], dev_a(k)))
         if h == 0:
             kloads[0].wait()
+            gram(0, 0, R)
     base += 2 * (A - 1)
     bcps = [None, None]
     pcps = [[], []]
@@ -249,7 +259,6 @@
             bcps[h].append(send(mine, mine, s1.at[n], r1.at[n], dev_b(k)))
         n = pbase + h * A
         pcps[h].append(send(mine, mine, s1.at[n], r1.at[n], partner))
-    gram(0)
     kloads[1].wait()
     loads[2].wait()
     loads[3].wait()
@@ -258,7 +267,8 @@
     def stack(i, carry):
         cols = pl.ds(pl.multiple_of(i * CH, CH), CH)
         parts = [gate_v[:, cols], up_v[:, cols], k_v[0, BASIS - 1, :, cols], k_v[1, BASIS - 1, :, cols]]
-        w4[:, cols] = jnp.concatenate([p.astype(F32) for p in parts], axis=0).astype(BF16)
+        w4t[cols, :] = jnp.concatenate([p.astype(F32) for p in parts], axis=0).T.astype(BF16)
+        downt[cols, :] = down_v[:, cols].astype(F32).T.astype(BF16)
         return carry
 
     lax.fori_loop(0, D // CH, stack, 0)
@@ -293,8 +303,6 @@
             ref = tok.at[h, c, back_of(b, k, A)]
             n = pbase + h * A + k
             pcps[h].append(send(ref, ref, s1.at[n], r1.at[n], partner))
-        if h == 0:
-            gram(1)
 
     every[...] = jnp.zeros_like(every)
     for h in range(2):
@@ -302,20 +310,20 @@
             cp.wait_recv()
 
         def first(i, carry, h=h):
-            cols = pl.ds(pl.multiple_of(i * CH, CH), CH)
-            half = tok[h, :, :, :, cols].reshape(T // 2, CH)
-            every[h] += mm_last(w4[:, cols], half)
+            cols = pl.ds(pl.multiple_of(i * CW, CW), CW)
+            half = tok[h, :, :, :, cols].reshape(T // 2, CW)
+            every[h] += mm(half, w4t[cols, :])
             return carry
 
-        lax.fori_loop(0, D // CH, first, 0)
-    whole = jnp.concatenate([every[0], every[1]], axis=1)
+        lax.fori_loop(0, D // CW, first, 0, unroll=True)
+    whole = jnp.concatenate([every[0], every[1]], axis=0)
     moved = None
     for _ in range(3):
         term = whole.astype(BF16)
         whole = whole - term.astype(F32)
-        term = mm_last(term, sel[...])
+        term = mm(sel[...], term)
         moved = term if moved is None else moved + term
-    pre[...] = moved
+    pre[...] = moved.T
     gate_pre = pre[0:F]
     up_pre = pre[F : 2 * F]
     tan_gate = pre[2 * F : 3 * F] * inv_d
@@ -323,6 +331,9 @@
     act, slope = gelu_pair(gate_pre)
     hidden = act * up_pre
     tangent = slope * tan_gate * up_pre + act * tan_up
+    act_v[...] = act
+    bend_v[...] = up_pre * slope
+    hid_v[...] = hidden.astype(BF16)
     hid_t = hidden.T.astype(BF16)
     tan_t = tangent.T.astype(BF16)
     kloads[2].wait()
@@ -356,7 +367,7 @@
         pass_a(1, k, total[HL:L])
     for k in order:
         pass_a(0, k, own[k, 0:HL, :])
-    gram(2)
+    gram(1, 0, R)
     base += 2 * (A - 1)
     bcps = [[], []]
     for h in halves:
@@ -386,9 +397,9 @@
         zsum[rows, :] = total
         for g in range(max(1, h * HZ), (h + 1) * HZ):
             k = NEAR[g]
-            zcps.append(
-                send(zsum.at[pl.ds(g * RZ, RZ)], zrecv.at[k - 1], s2.at[base + k], r2.at[base + k], dev_z(k))
-            )
+            start = (g - h * HZ) * RZ
+            zsend[g] = total[start : start + RZ].astype(BF16)
+            zcps.append(send(zsend.at[g], zrecv.at[k - 1], s2.at[base + k], r2.at[base + k], dev_z(k)))
     def keep(i, carry):
         cols = pl.ds(pl.multiple_of(i * CH, CH), CH)
         nc[:, cols] = mm(sel[...], tok[:, :, :, :, cols].reshape(T, CH)).astype(BF16)
@@ -399,7 +410,7 @@
         cp.wait_recv()
     total = zsum[0:RZ, :]
     for j in range(Z - 1):
-        total = total + zrecv[j]
+        total = total + zrecv[j].astype(F32)
     lz[0] = total.astype(BF16)
 
     zcps = {}
@@ -407,104 +418,126 @@
         g = SLOT[Z - k]
         zcps[g] = send(lz.at[0], lz.at[g], s3.at[g], r3.at[g], dev_z(k))
     base = Z
-    abase = base + 2 * (A - 1)
-    pbase = abase + 2 * A * (A - 1)
-    bcps = [[], []]
-    acps = {}
+    abase = base + NS * (A - 1)
+    pbase = abase + NS * 2 * (A - 1)
+    bcps = [[] for _ in range(NS)]
+    acps = [[] for _ in range(NS)]
     pcps = []
 
-    def pass_on(h, kb):
-        ref = loss.at[h, c, a, back_of(b, kb, A)]
-        for k in range(1, A):
-            n = abase + (h * A + kb) * (A - 1) + k - 1
-            acps[h, kb, k] = send(ref, ref, s3.at[n], r3.at[n], dev_a(k))
-        n = pbase + h * (2 * A - 1) + kb
-        pcps.append(send(ref, ref, s3.at[n], r3.at[n], partner))
-
-    for h in range(2):
-        for g in range(max(1, h * HZ), (h + 1) * HZ):
+    def build(h):
+        for g in range(max(1, h * G), (h + 1) * G):
             zcps[g].wait_recv()
-        groups = [lz[g].astype(F32) for g in range(h * HZ, (h + 1) * HZ)]
+        groups = [lz[g].astype(F32) for g in range(h * G, (h + 1) * G)]
         mine = groups[0] if len(groups) == 1 else jnp.concatenate(groups, axis=0)
-        loss[h, c, a, b] = mine.astype(BF16)
-        ref = loss.at[h, c, a, b]
+        loss[h, c, 0, 0] = mine.astype(BF16)
+        ref = loss.at[h, c, 0, 0]
         for k in range(1, A):
             n = base + h * (A - 1) + k - 1
-            bcps[h].append(send(ref, ref, s3.at[n], r3.at[n], dev_b(k)))
-        pass_on(h, 0)
-    for h in range(2):
-        for kb in range(1, A):
-            bcps[h][kb - 1].wait_recv()
-            pass_on(h, kb)
-    for h in range(2):
+            bcps[h].append(send(ref, loss.at[h, c, 0, k], s3.at[n], r3.at[n], dev_b(k)))
         for k in range(1, A):
-            for kb in range(A):
-                acps[h, kb, k].wait_recv()
-            ref = loss.at[h, c, back_of(a, k, A)]
-            n = pbase + h * (2 * A - 1) + A + k - 1
-            pcps.append(send(ref, ref, s3.at[n], r3.at[n], partner))
-    backacc[...] = jnp.zeros_like(backacc)
-    PER = CH // 128
-
-    def loss_cols(i):
-        halves = []
-        for h in range(2):
-            blocks = []
-            for j in range(PER):
-                n = i * PER + j
-                blocks.append(loss[h, n // (A * A), lax.rem(n // A, A), lax.rem(n, A)])
-            halves.append(jnp.concatenate(blocks, axis=1))
-        return jnp.concatenate(halves, axis=0)
-
-    def second_pass(i, carry):
-        cols = pl.ds(pl.multiple_of(i * CH, CH), CH)
-        backacc[...] += mm_last(down_v[:, cols], loss_cols(i))
-        return carry
-
-    count = D // CH // 2
-    lax.fori_loop(c * count, c * count + count, second_pass, 0)
-    for cp in pcps:
-        cp.wait_recv()
-    lax.fori_loop((1 - c) * count, (1 - c) * count + count, second_pass, 0)
-    back = backacc[...]
-    gate_pre = pre[0:F]
-    up_pre = pre[F : 2 * F]
-    act, slope = gelu_pair(gate_pre)
-    hid = (act * up_pre).astype(BF16)
-    both = jnp.concatenate([back * up_pre * slope, back * act], axis=0).astype(BF16)
-
-    def grads(i, carry):
-        cols = pl.ds(pl.multiple_of(i * CH, CH), CH)
-        two = mm(both, nc[:, cols]) * inv_d
-        three = mm(hid, loss_cols(i)) * inv_ff
-        parts = (two[0:F], two[F : 2 * F], three)
-        carry = list(carry)
-        for part in range(3):
-            grad = parts[part]
-            w_v[part, :, cols] = grad
-            for sub in range(CH // 128):
-                g = grad[:, sub * 128 : (sub + 1) * 128]
-                scols = pl.ds(pl.multiple_of(i * CH + sub * 128, 128), 128)
-                for j in range(BASIS):
-                    carry[j] = carry[j] + fold(k_v[part, j, :, scols].astype(F32) * g)
-                carry[BASIS] = carry[BASIS] + fold(g * g)
-        return tuple(carry)
-
-    zero = jnp.zeros((8, 128), F32)
-    sums = lax.fori_loop(0, D // CH, grads, (zero,) * (BASIS + 1))
+            n = abase + h * 2 * (A - 1) + k - 1
+            acps[h].append(send(ref, loss.at[h, c, k, 0], s3.at[n], r3.at[n], dev_a(k)))
+
+    def spread(h):
+        for cp in bcps[h]:
+            cp.wait_recv()
+        rest = pl.ds(1, A - 1)
+        for k in range(1, A):
+            n = abase + (h * 2 + 1) * (A - 1) + k - 1
+            acps[h].append(
+                send(loss.at[h, c, 0, rest], loss.at[h, c, k, rest], s3.at[n], r3.at[n], dev_a(k))
+            )
+        ref = loss.at[h, c, 0]
+        n = pbase + h * A
+        pcps.append(send(ref, ref, s3.at[n], r3.at[n], partner))
+
+    gram(2, 0, R // 2)
+    build(0)
+    gram(2, R // 2, R)
     qrows[...] = jnp.zeros_like(qrows)
-    for j in range(BASIS + 1):
-        qrows[j : j + 1, :] = jnp.sum(sums[j], axis=0, keepdims=True)
+    drows[...] = jnp.zeros_like(drows)
     n = 0
     for i1 in range(BASIS):
         for j1 in range(i1, BASIS):
             q = GRAM + i1 * BASIS + j1
             qrows[q : q + 1, :] = jnp.sum(gacc[n], axis=0, keepdims=True)
             n += 1
-    line = jnp.sum(qrows[...], axis=1, keepdims=True) * inv_count
-    rowi = lax.broadcasted_iota(jnp.int32, (128, 128), 0)
-    coli = lax.broadcasted_iota(jnp.int32, (128, 128), 1)
-    tile = jnp.sum(jnp.where(rowi == coli, line, 0.0), axis=0, keepdims=True)
+
+    def to_lanes(rows):
+        line = jnp.sum(rows[...], axis=1, keepdims=True) * inv_count
+        shape = rows.shape
+        rowi = lax.broadcasted_iota(jnp.int32, shape, 0)
+        coli = lax.broadcasted_iota(jnp.int32, shape, 1)
+        return jnp.sum(jnp.where(rowi == coli, line, 0.0), axis=0, keepdims=True)
+
+    gram_tile = to_lanes(qrows)
+    for h in range(1, NS):
+        build(h)
+    for h in range(NS):
+        spread(h)
+    for h in range(NS):
+        for k in range(1, A):
+            acps[h][k - 1].wait_recv()
+            acps[h][A - 1 + k - 1].wait_recv()
+            ref = loss.at[h, c, k]
+            n = pbase + h * A + k
+            pcps.append(send(ref, ref, s3.at[n], r3.at[n], partner))
+
+    backacc[...] = jnp.zeros_like(backacc)
+
+    def loss_cols(i, width):
+        bands = []
+        for h in range(NS):
+            blocks = []
+            for j in range(width // 128):
+                n = i * (width // 128) + j
+                side = n // (A * A)
+                other = side + c - 2 * side * c
+                ka = lax.rem(a + other * (b - a) + A - lax.rem(n // A, A), A)
+                kb = lax.rem(b + other * (a - b) + A - lax.rem(n, A), A)
+                blocks.append(loss[h, side, ka, kb])
+            bands.append(jnp.concatenate(blocks, axis=1))
+        return jnp.concatenate(bands, axis=0)
+
+    def second_pass(i, carry):
+        cols = pl.ds(pl.multiple_of(i * CW, CW), CW)
+        backacc[...] += mm(loss_cols(i, CW), downt[cols, :])
+        return carry
+
+    def dots(part, grad, i, carry):
+        carry = list(carry)
+        w_v[part, :, pl.ds(pl.multiple_of(i * CH, CH), CH)] = grad
+        for sub in range(CH // 128):
+            g = grad[:, sub * 128 : (sub + 1) * 128]
+            scols = pl.ds(pl.multiple_of(i * CH + sub * 128, 128), 128)
+            for j in range(BASIS):
+                carry[j] = carry[j] + fold(k_v[part, j, :, scols].astype(F32) * g)
+            carry[BASIS] = carry[BASIS] + fold(g * g)
+        return tuple(carry)
+
+    def third(i, carry):
+        return dots(2, mm(hid_v[...], loss_cols(i, CH)) * inv_ff, i, carry)
+
+    zero = jnp.zeros((8, 128), F32)
+    count = D // CW // 2
+    for i in range(count):
+        second_pass(c * count + i, 0)
+    for cp in pcps:
+        cp.wait_recv()
+    for i in range(count):
+        second_pass((1 - c) * count + i, 0)
+    back = backacc[...].T
+    both = jnp.concatenate([back * bend_v[...], back * act_v[...]], axis=0).astype(BF16)
+
+    def grads(i, carry):
+        cols = pl.ds(pl.multiple_of(i * CH, CH), CH)
+        two = mm(both, nc[:, cols]) * inv_d
+        return third(i, dots(1, two[F : 2 * F], i, dots(0, two[0:F], i, carry)))
+
+    sums = lax.fori_loop(0, D // CH, grads, (zero,) * (BASIS + 1), unroll=2)
+    for j in range(BASIS + 1):
+        drows[j : j + 1, :] = jnp.sum(sums[j], axis=0, keepdims=True)
+    tile = gram_tile + to_lanes(drows)
 
     def share(slots, value, at, devs, base):
         slots[at] = value
@@ -562,7 +595,7 @@
             out_v[part, :, cols] = (left_over * inv_norm).astype(BF16)
             return carry
 
-        lax.fori_loop(0, D // 256, final, 0)
+        lax.fori_loop(0, D // 256, final, 0, unroll=2)
         cp = pltpu.make_async_copy(out_v.at[part], dst, osem.at[part])
         cp.start()
         outs.append(cp)
@@ -584,11 +617,12 @@
     W = H // A
     HZ = Z // 2
     HL = L // 2
+    NS = min(2, Z)
     cfg = (Z, A, D, T, L, F, BASIS)
     pairs = BASIS * (BASIS + 1) // 2
     n1 = Z + 4 * (A - 1) + 2 * A
     n2 = A + 4 * (A - 1) + Z
-    n3 = Z + 2 * (A - 1) + 2 * A * (A - 1) + 2 * (2 * A - 1)
+    n3 = Z + NS * (A - 1) + NS * 2 * (A - 1) + NS * A
     n4 = 2 * Z - 1 + A * A - 1
     hbm = pl.BlockSpec(memory_space=pltpu.HBM)
     vmem = pl.BlockSpec(memory_space=pltpu.VMEM)
@@ -612,10 +646,11 @@
             pltpu.VMEM((Z, A, R, 128), BF16),
             pltpu.VMEM((HZ * A * R, 128), F32),
             pltpu.VMEM((2, 2, A, HZ * A, D), BF16),
-            pltpu.VMEM((4 * F, D), BF16),
+            pltpu.VMEM((D, 4 * F), BF16),
+            pltpu.VMEM((D, F), BF16),
             pltpu.VMEM((L, T), BF16),
             pltpu.VMEM((L, D), BF16),
-            pltpu.VMEM((2, 4 * F, T // 2), F32),
+            pltpu.VMEM((2, T // 2, 4 * F), F32),
             pltpu.VMEM((4 * F, L), F32),
             pltpu.VMEM((A, L, W), BF16),
             pltpu.VMEM((A, L, W), BF16),
@@ -625,12 +660,17 @@
             pltpu.VMEM((2, A - 1, HL, 128), BF16),
             pltpu.VMEM((2, A - 1, HL, 128), BF16),
             pltpu.VMEM((L, 128), F32),
-            pltpu.VMEM((Z - 1, L // Z, 128), F32),
             pltpu.VMEM((Z, L // Z, 128), BF16),
-            pltpu.VMEM((2, 2, A, A, HL, 128), BF16),
-            pltpu.VMEM((F, L), F32),
+            pltpu.VMEM((Z - 1, L // Z, 128), BF16),
+            pltpu.VMEM((Z, L // Z, 128), BF16),
+            pltpu.VMEM((NS, 2, A, A, L // NS, 128), BF16),
+            pltpu.VMEM((L, F), F32),
             pltpu.VMEM((pairs, 8, 128), F32),
             pltpu.VMEM((128, 128), F32),
+            pltpu.VMEM((16, 128), F32),
+            pltpu.VMEM((F, L), F32),
+            pltpu.VMEM((F, L), F32),
+            pltpu.VMEM((F, L), BF16),
             pltpu.VMEM((2 * Z, 1, 128), F32),
             pltpu.VMEM((A * A, 1, 128), F32),
             dma((5,)),

time: 83.2 us -> 81.5 us (0.980)
  Pallas kernels: 82.4 us -> 80.7 us
    pallas_call x1, Pallas kernels: 78.9 us -> 77.3 us  [per_device(): pl.pallas_call(functools.partial(body, cfg), out_shape=(pltpu.VMEM((3, F,...]
where the time goes in v3:
time: 81.5 us; the launch traced here: 81.3 us
  Pallas kernels  80.7 us (99%)
    pallas_call x1, Pallas kernels, per_device(): pl.pallas_call(functools.partial(body, cfg), out_shape=(pltpu.VMEM((3, F,...  77.3 us
    pallas_call x1, Pallas kernels, per_device(): pl.pallas_call(functools.partial(finish, (D, F, BASIS)), out_shape=(part,...  3.39 us

profile of v3, /device:TPU:1, one launch (start us, length us, event | category | flops | bytes accessed | tf_op | source)
XLA Modules:
  0.0 81.3 jit_solution(1050249201835297180)
XLA Ops:
  0.6 77.3 %arnoldi_step.1 = (f32[3,40,4096]{2,1,0:T(8,128)S(1)}, bf16[3,8,40,4096]{3,2,1,0:T(8,128)(2,1)S(1)}, f32[1,128]{1,0:T(1,128)S(1)}) custom-call(s32[2]{0:T(128)} %len_ref.1, bf16[1,4096]{1,0:T(2,128)(2,1)} %x_hbm.1, bf16[32,128]{1,0:T(8,128)(2,1)} %bitcast.1, bf16[40,4096]{1,0:T(8,128)(2,1)} %gate_hbm.1, bf16[40,4096]{1,0:T(8,128)(2,1)} %up_hbm.1, ...), custom_call_target="tpu_custom_call" | custom-call | tf_op jit(solution)/shard_map/arnoldi_step/pallas_call | solution.py:630
  77.9 3.4 %arnoldi_finish.1 = (bf16[40,4096]{1,0:T(8,128)(2,1)}, bf16[40,4096]{1,0:T(8,128)(2,1)}, bf16[40,4096]{1,0:T(8,128)(2,1)}, f32[9]{0:T(128)}) custom-call(f32[1,128]{1,0:T(1,128)S(1)} %get-tuple-element.7.coef_in, f32[3,40,4096]{2,1,0:T(8,128)S(1)} %get-tuple-element.8.w_v, bf16[3,8,40,4096]{3,2,1,0:T(8,128)(2,1)S(1)} %get-tuple-element.9.k_v), custom_call_target="tpu_custom_call" | custom-call | tf_op jit(solution)/shard_map/arnoldi_finish/pallas_call | solution.py:703
